TPU v7x, 32 devices: a whole 2x2x4 slice. The times are simulated.
32 devices in a mesh: parts: 1, row: 16 (over z, y, x), chan: 1, sub: 2 (over core).
Axes of the slice: x: 2, y: 2, z: 4, core: 2. Of those that a mesh axis runs over, the one named last changes fastest.
Arguments:
- pair: bfloat16 [448, 448, 128], P(('parts', 'row', 'sub'), 'chan'), may hold values from -6 to 6
- pair_mask: int32 [448, 448], P(('parts', 'row', 'sub'), 'chan'), may hold values 0 or 1
- out_in_gain: float32 [128], replicated, may hold values from 0.5 to 1.5
- out_proj: bfloat16 [128, 640], replicated, may hold values from -0.5 to 0.5
- out_mid_gain: float32 [128], replicated, may hold values from 0.5 to 1.5
- out_final: bfloat16 [128, 128], replicated, may hold values from -0.5 to 0.5
- in_in_gain: float32 [128], replicated, may hold values from 0.5 to 1.5
- in_proj: bfloat16 [128, 640], replicated, may hold values from -0.5 to 0.5
- in_mid_gain: float32 [128], replicated, may hold values from 0.5 to 1.5
- in_final: bfloat16 [128, 128], replicated, may hold values from -0.5 to 0.5
Outputs:
- updated: bfloat16 [448, 448, 128], P(('parts', 'row', 'sub'), 'chan')
All inputs are finite; a program needn't handle non-finite values. No bound on the sum of `pair_mask` on one device may be relied on, other than what follows from the above.
Results may differ from a plain program's by a relative error of at most 0.014.
Values may be sent and summed in bfloat16 or wider, within the bound.
A program may use at most 192 MiB of HBM per device.

v0:
```python
import jax
import jax.numpy as jnp
from jax import lax
from jax.sharding import PartitionSpec as P


def norm_last(values, gain):
    mean = jnp.mean(values, axis=-1, keepdims=True)
    var = jnp.mean((values - mean) ** 2, axis=-1, keepdims=True)
    return (values - mean) / jnp.sqrt(var + 1e-05) * gain


def project(pair, pair_mask, in_gain, proj, left_form, right_form, left_across):
    hidden = (proj.shape[1] - pair.shape[2]) // 4
    normed = norm_last(pair.astype(jnp.float32), in_gain).astype(jnp.bfloat16)
    keep = pair_mask.astype(jnp.float32)
    left_raw = jnp.einsum(
        left_form, normed, proj[:, : 2 * hidden], preferred_element_type=jnp.float32
    )
    right_raw = jnp.einsum(
        right_form, normed, proj[:, 2 * hidden : 4 * hidden], preferred_element_type=jnp.float32
    )
    left_keep = keep.T[None] if left_across else keep[None]
    left = (jax.nn.sigmoid(left_raw[:hidden]) * left_raw[hidden:] * left_keep).astype(jnp.bfloat16)
    right = (jax.nn.sigmoid(right_raw[:hidden]) * right_raw[hidden:] * keep[None]).astype(
        jnp.bfloat16
    )
    gate = jax.nn.sigmoid(
        jnp.dot(normed, proj[:, 4 * hidden :], preferred_element_type=jnp.float32)
    )
    return (left, right, gate)


def finish(pair, product, gate, mid_gain, final):
    group = product.shape[0]
    total = group * lax.axis_size("chan")
    first, second = (
        lax.psum(jnp.sum(product, axis=0).astype(jnp.bfloat16), "chan").astype(jnp.float32),
        lax.psum(jnp.sum(product * product, axis=0).astype(jnp.bfloat16), "chan").astype(
            jnp.float32
        ),
    )
    mean = first / total
    var = second / total - mean * mean
    offset = lax.axis_index("chan") * group
    gain_part = lax.dynamic_slice_in_dim(mid_gain, offset, group, 0)
    final_part = lax.dynamic_slice_in_dim(final, offset, group, 0)
    normed = ((product - mean) / jnp.sqrt(var + 1e-05) * gain_part[:, None, None]).astype(
        jnp.bfloat16
    )
    summed = lax.psum_scatter(
        jnp.einsum("crj,cd->jrd", normed, final_part, preferred_element_type=jnp.float32).astype(
            jnp.bfloat16
        ),
        "chan",
        scatter_dimension=0,
        tiled=True,
    ).astype(jnp.float32)
    update = jnp.transpose(summed, (1, 0, 2))
    return (pair.astype(jnp.float32) + gate * update).astype(jnp.bfloat16)


def shards(
    pair,
    pair_mask,
    out_in_gain,
    out_proj,
    out_mid_gain,
    out_final,
    in_in_gain,
    in_proj,
    in_mid_gain,
    in_final,
):
    left, right, gate = project(
        pair, pair_mask, out_in_gain, out_proj, "rqd,de->erq", "rqd,de->erq", False
    )
    left, right = (
        lax.all_to_all(left, "chan", split_axis=0, concat_axis=2, tiled=True),
        lax.all_to_all(right, "chan", split_axis=0, concat_axis=2, tiled=True),
    )
    product = jnp.einsum(
        "cik,cjk->cij",
        left,
        lax.all_gather(right, ("row", "sub"), axis=1, tiled=True),
        preferred_element_type=jnp.float32,
    )
    middle = finish(pair, product, gate, out_mid_gain, out_final)
    left_in, right_in, gate_in = project(
        middle, pair_mask, in_in_gain, in_proj, "rqd,de->eqr", "rqd,de->erq", True
    )
    columns = lax.all_to_all(
        lax.all_to_all(left_in, "chan", split_axis=0, concat_axis=1, tiled=True),
        ("row", "sub"),
        split_axis=1,
        concat_axis=2,
        tiled=True,
    )
    right_in = lax.all_to_all(right_in, "chan", split_axis=0, concat_axis=2, tiled=True)
    product_in = jnp.einsum(
        "cik,ckj->cij",
        columns,
        lax.all_gather(right_in, ("row", "sub"), axis=1, tiled=True),
        preferred_element_type=jnp.float32,
    )
    return finish(middle, product_in, gate_in, in_mid_gain, in_final)


def solution(mesh):
    placed = (
        P(("parts", "row", "sub"), "chan", None),
        P(("parts", "row", "sub"), "chan"),
        P(),
        P(),
        P(),
        P(),
        P(),
        P(),
        P(),
        P(),
    )
    return jax.shard_map(
        shards,
        mesh=mesh,
        in_specs=placed,
        out_specs=P(("parts", "row", "sub"), "chan", None),
        check_vma=False,
    )
```

profile of v0, /device:TPU:0, one launch (start us, length us, event | category | flops | bytes accessed | tf_op | source)
XLA Modules:
  0.0 842.3 jit_solution(12634183757078182451)
XLA Ops:
  6.5 0.0 copy-start
  6.5 0.0 all-gather.3.cloned.1.call-start
  6.6 2.1 convert_reduce_fusion.1
  8.7 3.1 fusion.7
  11.9 0.0 copy-done.2
  11.9 0.0 copy-done.12
  11.9 0.0 copy-done.10
  11.9 1.9 convolution_bitcast_fusion.3
  13.8 0.0 copy-start.7
  13.8 1.9 convolution_bitcast_fusion.2
  15.6 0.0 copy-done.7
  15.7 2.9 fusion.23
  18.6 0.0 all-gather.3.cloned.1.call-update
  18.6 0.2 all-gather.5.cloned.1.call-start
  18.9 3.2 copy.24
  22.1 279.2 %all-gather.3.cloned.1.call-done = bf16[128,448,448]{0,2,1:T(8,128)(2,1)} async-done(((bf16[128,14,448]{0,2,1:T(8,128)(2,1)}), bf16[128,448,448]{0,2,1:T(8,128)(2,1)}) %all-gather.3.cloned.1.call-update) | async-done | bytes 51380240 | tf_op jit(solution)/shard_map/all_gather | solution.py:85
  301.4 79.1 %copy.25 = bf16[128,448,448]{2,1,0:T(8,128)(2,1)} copy(bf16[128,448,448]{0,2,1:T(8,128)(2,1)} %all-gather.3.cloned.1.call-done) | data formatting | bytes 102760448 | tf_op jit(solution)/shard_map/all_gather | solution.py:85
  380.5 23.2 %fusion.63 = (bf16[14,448]{1,0:T(8,128)(2,1)S(1)}, bf16[14,448]{1,0:T(8,128)(2,1)S(1)}, f32[128,14,448]{2,1,0:T(8,128)S(1)}) fusion(bf16[128,14,448]{2,1,0:T(8,128)(2,1)} %copy.24, bf16[128,448,448]{2,1,0:T(8,128)(2,1)} %copy.25), kind=kOutput, calls=%fused_computation.84 | convolution fusion | flops 721719040 | bytes 56222208 | tf_op jit(solution)/shard_map/cik,cjk->cij/dot_general | solution.py:82
  403.7 0.0 copy-done.8
  403.7 0.5 multiply_convert_fusion.1
  404.2 0.0 copy-start.3
  404.2 2.2 fusion.36
  406.4 0.0 copy-start.11
  406.5 0.0 copy-start.13
  406.5 2.9 convert_reduce_fusion
  409.3 0.0 copy-start.4
  409.4 2.0 fusion.4
  411.4 1.9 convolution_bitcast_fusion
  413.3 1.9 fusion.13
  415.2 0.0 all-gather.5.cloned.1.call-update
  415.2 1.9 convolution_bitcast_fusion.1
  417.1 1.4 fusion.18
  418.5 1.1 copy.27
  419.6 80.0 %all_to_all.18 = bf16[128,448,14]{0,2,1:T(8,128)(2,1)S(1)} all-to-all(bf16[128,448,14]{0,2,1:T(8,128)(2,1)S(1)} %copy.27), channel_id=1, replica_groups=mesh['parts'=1,'row'=16,'chan'=1,'sub'=2] {'row','sub'}, dimensions={1} | all-to-all | bytes 3211264 | tf_op jit(solution)/shard_map/all_to_all | solution.py:92
  499.6 0.5 copy.29
  500.0 1.4 all_to_all.16
  501.4 3.7 copy.30
  505.1 224.0 %all-gather.5.cloned.1.call-done = bf16[128,448,448]{0,2,1:T(8,128)(2,1)} async-done(((bf16[128,14,448]{0,2,1:T(8,128)(2,1)}), bf16[128,448,448]{0,2,1:T(8,128)(2,1)}) %all-gather.5.cloned.1.call-update) | async-done | bytes 51380240 | tf_op jit(solution)/shard_map/all_gather | solution.py:103
  729.1 79.1 %copy.31 = bf16[128,448,448]{2,1,0:T(8,128)(2,1)} copy(bf16[128,448,448]{0,2,1:T(8,128)(2,1)} %all-gather.5.cloned.1.call-done) | data formatting | bytes 102760448 | tf_op jit(solution)/shard_map/all_gather | solution.py:103
  808.2 20.7 %fusion.62 = (bf16[14,448]{1,0:T(8,128)(2,1)S(1)}, bf16[14,448]{1,0:T(8,128)(2,1)S(1)}, f32[128,14,448]{2,1,0:T(8,128)S(1)}) fusion(bf16[128,14,448]{2,1,0:T(8,128)(2,1)S(1)} %copy.30, bf16[128,448,448]{2,1,0:T(8,128)(2,1)} %copy.31), kind=kOutput, calls=%fused_computation.83 | convolution fusion | flops 721719040 | bytes 56222208 | tf_op jit(solution)/shard_map/cik,ckj->cij/dot_general | solution.py:100
  829.0 0.0 copy-start.6
  829.0 0.5 multiply_convert_fusion
  829.5 0.2 copy-done.6
  829.7 2.2 fusion.39
  831.9 0.0 copy-done.5
  831.9 0.0 copy-start.1
  831.9 3.5 fusion.11
  835.4 0.0 copy-done.1
  (19 shorter events, 0.1 us)
Async XLA Ops:
  6.5 397.7 %copy-start = (bf16[128,128]{1,0:T(8,128)(2,1)S(1)}, bf16[128,128]{1,0:T(8,128)(2,1)}, u32[]{:S(2)}) copy-start(bf16[128,128]{1,0:T(8,128)(2,1)} %param.15) | copy-start | bytes 98308
  6.5 5.3 copy-start.2
  6.5 5.3 copy-start.12
  6.5 5.4 copy-start.10
  6.5 294.8 %all-gather.3.cloned.1.call-start = ((), (), s32[]{:S(2)}) async-start(), calls=%async_computation.1 | async-start | bytes 52985856 | tf_op jit(solution)/shard_map/all_gather | solution.py:85
  13.8 1.9 copy-start.7
  18.6 710.5 %all-gather.5.cloned.1.call-start = ((), (), s32[]{:S(2)}) async-start(), calls=%async_computation.2 | async-start | bytes 52985856 | tf_op jit(solution)/shard_map/all_gather | solution.py:103
  380.5 23.2 %copy-start.8 = (f32[128]{0:T(128)S(1)}, f32[128]{0:T(128)}, u32[]{:S(2)}) copy-start(f32[128]{0:T(128)} %param.14) | copy-start | bytes 1540
  404.2 2.2 copy-start.3
  406.4 5.0 copy-start.11
  406.5 5.0 copy-start.13
  409.3 5.9 copy-start.4
  808.2 20.8 %copy-start.9 = (f32[128]{0:T(128)S(1)}, f32[128]{0:T(128)}, u32[]{:S(2)}) copy-start(f32[128]{0:T(128)} %param.18) | copy-start | bytes 1540
  829.0 0.8 copy-start.6
  829.7 2.2 copy-start.5
  831.9 3.5 copy-start.1
Sparse Core Ops, SparseCore 0:
  18.8 282.5 all-gather.2
  415.4 313.7 all-gather.4
where the time goes:
time: 846 us; the launch traced here: 842 us
  waiting for transfers between devices  503 us (59%)
  local copies, waits for them, and re-layouts  168 us (20%)
  blocking collectives  80 us (9%)
  matrix products  62.1 us (7%)
  other arithmetic  14.6 us (2%)
  between operations  13.7 us (2%)
    all_gather x1, waiting for transfers between devices, shards(): lax.all_gather(right, ('row', 'sub'), axis=1, tiled=True)  279 us
    all_gather x1, waiting for transfers between devices, shards(): lax.all_gather(right_in, ('row', 'sub'), axis=1, tiled=True)  224 us
    all_to_all x1, blocking collectives, shards(): lax.all_to_all(lax.all_to_all(left_in, 'chan', split_axis=0, concat_axis=...  80 us
    all_gather x1, local copies, waits for them, and re-layouts, shards(): lax.all_gather(right, ('row', 'sub'), axis=1, tiled=True)  79.1 us
    all_gather x1, local copies, waits for them, and re-layouts, shards(): lax.all_gather(right_in, ('row', 'sub'), axis=1, tiled=True)  79.1 us
    dot_general x1, matrix products, shards(): jnp.einsum('cik,cjk->cij', left, lax.all_gather(right, ('row', 'sub'), ax...  23.2 us
    dot_general x1, matrix products, shards(): jnp.einsum('cik,ckj->cij', columns, lax.all_gather(right_in, ('row', 'sub...  20.7 us
  transfers between devices with their start and end apart: 2, of which 2 were waited for; matrix products, arithmetic and copies ran while one was open for 1% of the time, Pallas kernels for 0%

commit v1 on v0

--- a/solution.py
+++ b/solution.py
@@ -2,6 +2,11 @@
 import jax.numpy as jnp
 from jax import lax
 from jax.sharding import PartitionSpec as P
+
+
+def all_parts(x, axis, along):
+    blocks = lax.all_gather(x, axis)
+    return jnp.concatenate(blocks, axis=along)
 
 
 def norm_last(values, gain):
@@ -100,7 +105,7 @@
     product_in = jnp.einsum(
         "cik,ckj->cij",
         columns,
-        lax.all_gather(right_in, ("row", "sub"), axis=1, tiled=True),
+        all_parts(right_in, ("row", "sub"), 1),
         preferred_element_type=jnp.float32,
     )
     return finish(middle, product_in, gate_in, in_mid_gain, in_final)

time: 846 us -> 878 us (1.038)
  local copies, waits for them, and re-layouts: 168 us -> 203 us
  blocking collectives: 80 us -> 65.7 us
  waiting for transfers between devices: 503 us -> 515 us
    reshape x0 -> x1, local copies, waits for them, and re-layouts: none -> 79.1 us  [all_parts(): return jnp.concatenate(blocks, axis=along)]
    all_gather x1, local copies, waits for them, and re-layouts: 79.1 us -> 34.7 us  [all_parts(): blocks = lax.all_gather(x, axis)]
    all_to_all x1, blocking collectives: 80 us -> 65.7 us  [shards(): lax.all_to_all(lax.all_to_all(left_in, 'chan', split_axis=0, concat_axis=...]
    all_gather x1, waiting for transfers between devices: 224 us -> 235 us  [all_parts(): blocks = lax.all_gather(x, axis)]
where the time goes in v1:
time: 878 us; the launch traced here: 874 us
  waiting for transfers between devices  515 us (59%)
  local copies, waits for them, and re-layouts  203 us (23%)
  blocking collectives  65.7 us (7%)
  matrix products  62.1 us (7%)
  other arithmetic  14.6 us (2%)
  between operations  13.7 us (2%)
    all_gather x1, waiting for transfers between devices, shards(): lax.all_gather(right, ('row', 'sub'), axis=1, tiled=True)  279 us
    all_gather x1, waiting for transfers between devices, all_parts(): blocks = lax.all_gather(x, axis)  235 us
    reshape x1, local copies, waits for them, and re-layouts, all_parts(): return jnp.concatenate(blocks, axis=along)  79.1 us
    all_gather x1, local copies, waits for them, and re-layouts, shards(): lax.all_gather(right, ('row', 'sub'), axis=1, tiled=True)  79.1 us
    all_to_all x1, blocking collectives, shards(): lax.all_to_all(lax.all_to_all(left_in, 'chan', split_axis=0, concat_axis=...  65.7 us
    all_gather x1, local copies, waits for them, and re-layouts, all_parts(): blocks = lax.all_gather(x, axis)  34.7 us
    dot_general x1, matrix products, shards(): jnp.einsum('cik,cjk->cij', left, lax.all_gather(right, ('row', 'sub'), ax...  23.2 us
    dot_general x1, matrix products, shards(): jnp.einsum('cik,ckj->cij', columns, all_parts(right_in, ('row', 'sub'), 1...  20.7 us
  transfers between devices with their start and end apart: 2, of which 2 were waited for; matrix products, arithmetic and copies ran while one was open for 1% of the time, Pallas kernels for 0%

profile of v1, /device:TPU:0, one launch (start us, length us, event | category | flops | bytes accessed | tf_op | source)
XLA Modules:
  0.0 873.9 jit_solution(15426027458092962814)
XLA Ops:
  6.5 0.0 copy-start
  6.5 0.0 all-gather.4.cloned.1.call-start
  6.6 2.1 convert_reduce_fusion.1
  8.7 3.1 fusion.7
  11.9 0.0 copy-done.2
  11.9 0.0 copy-done.12
  11.9 0.0 copy-done.10
  11.9 1.9 convolution_bitcast_fusion.3
  13.8 0.0 copy-start.7
  13.8 1.9 convolution_bitcast_fusion.2
  15.6 0.0 copy-done.7
  15.7 2.9 fusion.23
  18.6 0.0 all-gather.4.cloned.1.call-update
  18.6 0.2 all-gather.6.cloned.1.call-start
  18.9 3.2 copy.25
  22.1 279.2 %all-gather.4.cloned.1.call-done = bf16[128,448,448]{0,2,1:T(8,128)(2,1)} async-done(((bf16[128,14,448]{0,2,1:T(8,128)(2,1)}), bf16[128,448,448]{0,2,1:T(8,128)(2,1)}) %all-gather.4.cloned.1.call-update) | async-done | bytes 51380240 | tf_op jit(solution)/shard_map/all_gather | solution.py:90
  301.4 79.1 %copy.26 = bf16[128,448,448]{2,1,0:T(8,128)(2,1)} copy(bf16[128,448,448]{0,2,1:T(8,128)(2,1)} %all-gather.4.cloned.1.call-done) | data formatting | bytes 102760448 | tf_op jit(solution)/shard_map/all_gather | solution.py:90
  380.5 23.2 %fusion.63 = (bf16[14,448]{1,0:T(8,128)(2,1)S(1)}, bf16[14,448]{1,0:T(8,128)(2,1)S(1)}, f32[128,14,448]{2,1,0:T(8,128)S(1)}) fusion(bf16[128,14,448]{2,1,0:T(8,128)(2,1)} %copy.25, bf16[128,448,448]{2,1,0:T(8,128)(2,1)} %copy.26), kind=kOutput, calls=%fused_computation.85 | convolution fusion | flops 721719040 | bytes 56222208 | tf_op jit(solution)/shard_map/cik,cjk->cij/dot_general | solution.py:87
  403.7 0.0 copy-done.8
  403.7 0.5 multiply_convert_fusion.1
  404.2 0.0 copy-start.3
  404.2 2.2 fusion.36
  406.4 0.0 copy-start.11
  406.5 0.0 copy-start.13
  406.5 2.9 convert_reduce_fusion
  409.3 0.0 copy-start.4
  409.4 2.0 fusion.4
  411.4 1.9 convolution_bitcast_fusion
  413.3 1.9 fusion.13
  415.2 0.0 all-gather.6.cloned.1.call-update
  415.2 0.0 copy-done.4
  415.2 1.9 convolution_bitcast_fusion.1
  417.1 1.4 fusion.18
  418.5 1.1 copy.28
  419.6 65.7 %all_to_all.18 = bf16[128,448,14]{0,2,1:T(8,128)(2,1)S(1)} all-to-all(bf16[128,448,14]{0,2,1:T(8,128)(2,1)S(1)} %copy.28), channel_id=1, replica_groups=mesh['parts'=1,'row'=16,'chan'=1,'sub'=2] {'row','sub'}, dimensions={1} | all-to-all | bytes 3211264 | tf_op jit(solution)/shard_map/all_to_all | solution.py:97
  485.3 0.5 copy.30
  485.7 1.4 all_to_all.16
  487.2 3.5 copy.32
  490.7 235.3 %all-gather.6.cloned.1.call-done = bf16[4096,14,448]{0,2,1:T(8,128)(2,1)} async-done(((bf16[128,14,448]{0,2,1:T(8,128)(2,1)}), bf16[4096,14,448]{0,2,1:T(8,128)(2,1)}) %all-gather.6.cloned.1.call-update) | async-done | bytes 51380240 | tf_op jit(solution)/shard_map/all_gather | solution.py:8
  726.0 34.7 %copy_bitcast_fusion = bf16[32,128,14,448]{1,3,2,0:T(8,128)(2,1)} fusion(bf16[4096,14,448]{0,2,1:T(8,128)(2,1)} %all-gather.6.cloned.1.call-done), kind=kLoop, calls=%fused_computation | loop fusion | bytes 102760448 | tf_op jit(solution)/shard_map/all_gather | solution.py:8
  760.7 79.1 %copy.33 = bf16[128,448,448]{2,1,0:T(8,128)(2,1)} copy(bf16[128,448,448]{0,2,1:T(8,128)(2,1)} %bitcast.54) | data formatting | bytes 102760448 | tf_op jit(solution)/shard_map/reshape | solution.py:9
  839.8 20.7 %fusion.62 = (bf16[14,448]{1,0:T(8,128)(2,1)S(1)}, bf16[14,448]{1,0:T(8,128)(2,1)S(1)}, f32[128,14,448]{2,1,0:T(8,128)S(1)}) fusion(bf16[128,14,448]{2,1,0:T(8,128)(2,1)S(1)} %copy.32, bf16[128,448,448]{2,1,0:T(8,128)(2,1)} %copy.33), kind=kOutput, calls=%fused_computation.84 | convolution fusion | flops 721719040 | bytes 56222208 | tf_op jit(solution)/shard_map/cik,ckj->cij/dot_general | solution.py:105
  860.6 0.0 copy-start.6
  860.6 0.5 multiply_convert_fusion
  861.1 0.2 copy-done.6
  861.3 2.2 fusion.39
  863.5 0.0 copy-start.1
  863.5 3.5 fusion.11
  (20 shorter events, 0.1 us)
Async XLA Ops:
  6.5 397.7 %copy-start = (bf16[128,128]{1,0:T(8,128)(2,1)S(1)}, bf16[128,128]{1,0:T(8,128)(2,1)}, u32[]{:S(2)}) copy-start(bf16[128,128]{1,0:T(8,128)(2,1)} %param.15) | copy-start | bytes 98308
  6.5 5.3 copy-start.2
  6.5 5.3 copy-start.12
  6.5 5.4 copy-start.10
  6.5 294.8 %all-gather.4.cloned.1.call-start = ((), (), s32[]{:S(2)}) async-start(), calls=%async_computation.1 | async-start | bytes 52985856 | tf_op jit(solution)/shard_map/all_gather | solution.py:90
  13.8 1.9 copy-start.7
  18.6 707.3 %all-gather.6.cloned.1.call-start = ((), (), s32[]{:S(2)}) async-start(), calls=%async_computation.2 | async-start | bytes 52985856 | tf_op jit(solution)/shard_map/all_gather | solution.py:8
  380.5 23.2 %copy-start.8 = (f32[128]{0:T(128)S(1)}, f32[128]{0:T(128)}, u32[]{:S(2)}) copy-start(f32[128]{0:T(128)} %param.14) | copy-start | bytes 1540
  404.2 2.2 copy-start.3
  406.4 5.0 copy-start.11
  406.5 5.0 copy-start.13
  409.3 5.9 copy-start.4
  839.8 20.8 %copy-start.9 = (f32[128]{0:T(128)S(1)}, f32[128]{0:T(128)}, u32[]{:S(2)}) copy-start(f32[128]{0:T(128)} %param.18) | copy-start | bytes 1540
  860.6 0.8 copy-start.6
  861.3 2.2 copy-start.5
  863.5 3.5 copy-start.1
Sparse Core Ops, SparseCore 0:
  18.8 282.5 all-gather.3
  415.3 310.5 all-gather.5
